TPU v7x, 128 devices: a whole 4x4x4 slice. The times are simulated.
128 devices in a mesh: blk: 16 (over x_lo, y, core), head: 8 (over x_hi, z).
Axes of the slice: x: 4 (x_hi: 2, x_lo: 2; x = x_hi * 2 + x_lo), y: 4, z: 4, core: 2. Of those that a mesh axis runs over, the one named last changes fastest.
Arguments:
- queries: bfloat16 [16384, 3072], P(('blk', 'head')), may hold values from -100 to 100
- keys: bfloat16 [16384, 3072], P(('blk', 'head')), may hold values from -100 to 100
- values: bfloat16 [16384, 3072], P(('blk', 'head')), may hold values from -6 to 6
- query_gain: float32 [3072], replicated, may hold values from 1 to 4
- key_gain: float32 [3072], replicated, may hold values from 0.1 to 1.9
Outputs:
- attended: bfloat16 [16384, 3072], P(('blk', 'head'))
All inputs are finite; a program needn't handle non-finite values.
Results may differ from a plain program's by a relative error of at most 0.0075.
The roundings to bfloat16 on the way count: a program that leaves them out, or rounds other values in their place, can miss the bound.
Values may be sent and summed in bfloat16 or wider, within the bound.
A program may use at most 128 MiB of HBM per device.

v0:
```python
import math
import jax
import jax.numpy as jnp
from jax import lax
from jax.sharding import PartitionSpec as P

HEAD_DIM = 128


def normalize(block, gain):
    wide = block.astype(jnp.float32)
    mean_sq = jnp.mean(wide * wide, axis=-1, keepdims=True)
    return (wide * lax.rsqrt(mean_sq + 1e-06) * gain).astype(jnp.bfloat16)


def absorb(carry, pieces, q_heads, factor):
    run_max, run_sum, accum = carry
    key_block, value_block = pieces
    scores = (
        jnp.einsum("qhd,khd->hqk", q_heads, key_block, preferred_element_type=jnp.float32) * factor
    )
    new_max = jnp.maximum(run_max, jnp.max(scores, axis=-1))
    shrink = jnp.exp(run_max - new_max)
    weights = jnp.exp(scores - new_max[:, :, None])
    new_sum = run_sum * shrink + jnp.sum(weights, axis=-1)
    mixed = jnp.einsum(
        "hqk,khd->hqd",
        weights.astype(jnp.bfloat16),
        value_block,
        preferred_element_type=jnp.float32,
    )
    return (new_max, new_sum, accum * shrink[:, :, None] + mixed)


def shards(queries, keys, values, query_gain, key_gain):
    group = lax.axis_size("head")
    width = queries.shape[1] // group
    heads_here = width // HEAD_DIM
    factor = 1.0 / math.sqrt(HEAD_DIM)
    first_part = normalize(queries, query_gain)
    second_part = normalize(keys, key_gain)
    q_local, k_local, v_local = (
        lax.all_to_all(first_part, "head", split_axis=1, concat_axis=0, tiled=True),
        lax.all_to_all(second_part, "head", split_axis=1, concat_axis=0, tiled=True),
        lax.all_to_all(values, "head", split_axis=1, concat_axis=0, tiled=True),
    )
    rows = q_local.shape[0]
    q_heads = q_local.reshape(rows, heads_here, HEAD_DIM)
    k_heads = k_local.reshape(rows, heads_here, HEAD_DIM)
    v_heads = v_local.reshape(rows, heads_here, HEAD_DIM)
    start_state = (
        jnp.full((heads_here, rows), -jnp.inf, jnp.float32),
        jnp.zeros((heads_here, rows), jnp.float32),
        jnp.zeros((heads_here, rows, HEAD_DIM), jnp.float32),
    )
    key_piece = lax.all_gather(k_heads, "blk", axis=0, tiled=True)
    value_piece = lax.all_gather(v_heads, "blk", axis=0, tiled=True)
    length = key_piece.shape[0]
    block_rows = math.gcd(length, 1024)
    count = length // block_rows
    key_blocks = key_piece.reshape(count, block_rows, heads_here, HEAD_DIM)
    value_blocks = value_piece.reshape(count, block_rows, heads_here, HEAD_DIM)

    def step_fn(state, blocks):
        return (absorb(state, blocks, q_heads, factor), None)

    final_state, unused = lax.scan(step_fn, start_state, (key_blocks, value_blocks))
    run_max, run_sum, accum = final_state
    result = accum / run_sum[:, :, None]
    result = jnp.transpose(result, (1, 0, 2)).reshape(rows, width).astype(jnp.bfloat16)
    return lax.all_to_all(result, "head", split_axis=0, concat_axis=1, tiled=True)


def solution(mesh):
    placed = (
        P(("blk", "head"), None),
        P(("blk", "head"), None),
        P(("blk", "head"), None),
        P(),
        P(),
    )
    return jax.shard_map(
        shards, mesh=mesh, in_specs=placed, out_specs=P(("blk", "head"), None), check_vma=False
    )
```

profile of v0, /device:TPU:0, one launch (start us, length us, event | category | flops | bytes accessed | tf_op | source)
XLA Modules:
  0.0 578.3 jit_solution(14939098089677855722)
XLA Ops:
  9.7 22.0 %all_to_all.64 = bf16[128,8,384]{0,2,1:T(8,128)(2,1)S(1)} all-to-all(bf16[128,8,384]{0,2,1:T(8,128)(2,1)S(1)} %bitcast.64), channel_id=1, replica_groups=mesh['blk'=16,'head'=8] {'head'}, dimensions={1} | all-to-all | bytes 1572864 | tf_op jit(solution)/shard_map/all_to_all | solution.py:44
  33.9 21.0 %all_to_all.65 = bf16[128,8,384]{0,2,1:T(8,128)(2,1)S(1)} all-to-all(bf16[128,8,384]{0,2,1:T(8,128)(2,1)S(1)} %bitcast.70), channel_id=1, replica_groups=mesh['blk'=16,'head'=8] {'head'}, dimensions={1} | all-to-all | bytes 1572864 | tf_op jit(solution)/shard_map/all_to_all | solution.py:45
  62.2 18.7 %all-to-all-done.1 = bf16[128,8,384]{0,2,1:T(8,128)(2,1)S(1)} async-done(((bf16[128,8,384]{0,2,1:T(8,128)(2,1)}), bf16[128,8,384]{0,2,1:T(8,128)(2,1)S(1)}, u32[]{:S(2)}, u32[]{:S(2)}) %all-to-all-start.1) | async-done | bytes 786464 | tf_op jit(solution)/shard_map/all_to_all | solution.py:43
  82.8 31.2 %all-gather.3.cloned.1.call-done = bf16[16384,3,128]{0,2,1:T(8,128)(2,1)} async-done(((bf16[1024,3,128]{0,2,1:T(8,128)(2,1)}), bf16[16384,3,128]{0,2,1:T(8,128)(2,1)}) %all-gather.3.cloned.1.call-update) | async-done | bytes 12582928 | tf_op jit(solution)/shard_map/all_gather | solution.py:56
  114.0 16.7 %copy.32 = bf16[16384,3,128]{2,0,1:T(8,128)(2,1)} copy(bf16[16384,3,128]{0,2,1:T(8,128)(2,1)} %all-gather.3.cloned.1.call-done) | data formatting | bytes 25165824 | tf_op jit(solution)/shard_map/all_gather | solution.py:56
  130.7 59.0 %all-gather.5.cloned.1.call-done = bf16[16384,3,128]{0,2,1:T(8,128)(2,1)} async-done(((bf16[1024,3,128]{0,2,1:T(8,128)(2,1)}), bf16[16384,3,128]{0,2,1:T(8,128)(2,1)}) %all-gather.5.cloned.1.call-update) | async-done | bytes 12582928 | tf_op jit(solution)/shard_map/all_gather | solution.py:57
  189.6 16.6 %copy.37 = bf16[16384,3,128]{2,0,1:T(8,128)(2,1)} copy(bf16[16384,3,128]{0,2,1:T(8,128)(2,1)} %all-gather.5.cloned.1.call-done) | data formatting | bytes 25165824 | tf_op jit(solution)/shard_map/all_gather | solution.py:57
  206.2 340.2 %while.15 = (s32[]{:T(128)}, f32[3,1024]{1,0:T(4,128)S(1)}, f32[3,1024]{1,0:T(4,128)S(1)}, f32[3,1024,128]{2,1,0:T(8,128)}, bf16[16,1024,3,128]{3,1,0,2:T(8,128)...) while((s32[]{:T(128)}, f32[3,1024]{1,0:T(4,128)S(1)}, ...), condition=%wide.region_5.6_spmd.clone, body=%wide.region_2.5_spmd.clone.sunk | while | flops 1636973568 | bytes 93783168 | solution.py:67
  227.3 7.8 %bitcast_reduce_fusion.2 = (f32[3,1024]{1,0:T(4,128)S(1)}, f32[3,1024,1024]{2,1,0:T(8,128)}) fusion(bf16[1024,3,128]{2,0,1:T(8,128)(2,1)} %get-tuple-element.182, bf16[16,1024,3,128]{3,1,0,2:T(8,128)(2,1)} %get-tuple-element.181, s32[]{:T(128)} %get-tuple-element.168), kind=kOutput, calls=%fused_computation.1.clone.1 | convolution fusion | flops 811594752 | bytes 14168576 | tf_op jit(solution)/shard_map/while/body/eval_jaxpr/qhd,khd->hqk/dot_general | solution.py:20
  248.5 7.8 %bitcast_reduce_fusion.2 = (f32[3,1024]{1,0:T(4,128)S(1)}, f32[3,1024,1024]{2,1,0:T(8,128)}) fusion(bf16[1024,3,128]{2,0,1:T(8,128)(2,1)} %get-tuple-element.182, bf16[16,1024,3,128]{3,1,0,2:T(8,128)(2,1)} %get-tuple-element.181, s32[]{:T(128)} %get-tuple-element.168), kind=kOutput, calls=%fused_computation.1.clone.1 | convolution fusion | flops 811594752 | bytes 14168576 | tf_op jit(solution)/shard_map/while/body/eval_jaxpr/qhd,khd->hqk/dot_general | solution.py:20
  269.8 7.8 %bitcast_reduce_fusion.2 = (f32[3,1024]{1,0:T(4,128)S(1)}, f32[3,1024,1024]{2,1,0:T(8,128)}) fusion(bf16[1024,3,128]{2,0,1:T(8,128)(2,1)} %get-tuple-element.182, bf16[16,1024,3,128]{3,1,0,2:T(8,128)(2,1)} %get-tuple-element.181, s32[]{:T(128)} %get-tuple-element.168), kind=kOutput, calls=%fused_computation.1.clone.1 | convolution fusion | flops 811594752 | bytes 14168576 | tf_op jit(solution)/shard_map/while/body/eval_jaxpr/qhd,khd->hqk/dot_general | solution.py:20
  291.1 7.8 %bitcast_reduce_fusion.2 = (f32[3,1024]{1,0:T(4,128)S(1)}, f32[3,1024,1024]{2,1,0:T(8,128)}) fusion(bf16[1024,3,128]{2,0,1:T(8,128)(2,1)} %get-tuple-element.182, bf16[16,1024,3,128]{3,1,0,2:T(8,128)(2,1)} %get-tuple-element.181, s32[]{:T(128)} %get-tuple-element.168), kind=kOutput, calls=%fused_computation.1.clone.1 | convolution fusion | flops 811594752 | bytes 14168576 | tf_op jit(solution)/shard_map/while/body/eval_jaxpr/qhd,khd->hqk/dot_general | solution.py:20
  312.4 7.8 %bitcast_reduce_fusion.2 = (f32[3,1024]{1,0:T(4,128)S(1)}, f32[3,1024,1024]{2,1,0:T(8,128)}) fusion(bf16[1024,3,128]{2,0,1:T(8,128)(2,1)} %get-tuple-element.182, bf16[16,1024,3,128]{3,1,0,2:T(8,128)(2,1)} %get-tuple-element.181, s32[]{:T(128)} %get-tuple-element.168), kind=kOutput, calls=%fused_computation.1.clone.1 | convolution fusion | flops 811594752 | bytes 14168576 | tf_op jit(solution)/shard_map/while/body/eval_jaxpr/qhd,khd->hqk/dot_general | solution.py:20
  333.7 7.8 %bitcast_reduce_fusion.2 = (f32[3,1024]{1,0:T(4,128)S(1)}, f32[3,1024,1024]{2,1,0:T(8,128)}) fusion(bf16[1024,3,128]{2,0,1:T(8,128)(2,1)} %get-tuple-element.182, bf16[16,1024,3,128]{3,1,0,2:T(8,128)(2,1)} %get-tuple-element.181, s32[]{:T(128)} %get-tuple-element.168), kind=kOutput, calls=%fused_computation.1.clone.1 | convolution fusion | flops 811594752 | bytes 14168576 | tf_op jit(solution)/shard_map/while/body/eval_jaxpr/qhd,khd->hqk/dot_general | solution.py:20
  354.9 7.8 %bitcast_reduce_fusion.2 = (f32[3,1024]{1,0:T(4,128)S(1)}, f32[3,1024,1024]{2,1,0:T(8,128)}) fusion(bf16[1024,3,128]{2,0,1:T(8,128)(2,1)} %get-tuple-element.182, bf16[16,1024,3,128]{3,1,0,2:T(8,128)(2,1)} %get-tuple-element.181, s32[]{:T(128)} %get-tuple-element.168), kind=kOutput, calls=%fused_computation.1.clone.1 | convolution fusion | flops 811594752 | bytes 14168576 | tf_op jit(solution)/shard_map/while/body/eval_jaxpr/qhd,khd->hqk/dot_general | solution.py:20
  376.2 7.8 %bitcast_reduce_fusion.2 = (f32[3,1024]{1,0:T(4,128)S(1)}, f32[3,1024,1024]{2,1,0:T(8,128)}) fusion(bf16[1024,3,128]{2,0,1:T(8,128)(2,1)} %get-tuple-element.182, bf16[16,1024,3,128]{3,1,0,2:T(8,128)(2,1)} %get-tuple-element.181, s32[]{:T(128)} %get-tuple-element.168), kind=kOutput, calls=%fused_computation.1.clone.1 | convolution fusion | flops 811594752 | bytes 14168576 | tf_op jit(solution)/shard_map/while/body/eval_jaxpr/qhd,khd->hqk/dot_general | solution.py:20
  397.5 7.8 %bitcast_reduce_fusion.2 = (f32[3,1024]{1,0:T(4,128)S(1)}, f32[3,1024,1024]{2,1,0:T(8,128)}) fusion(bf16[1024,3,128]{2,0,1:T(8,128)(2,1)} %get-tuple-element.182, bf16[16,1024,3,128]{3,1,0,2:T(8,128)(2,1)} %get-tuple-element.181, s32[]{:T(128)} %get-tuple-element.168), kind=kOutput, calls=%fused_computation.1.clone.1 | convolution fusion | flops 811594752 | bytes 14168576 | tf_op jit(solution)/shard_map/while/body/eval_jaxpr/qhd,khd->hqk/dot_general | solution.py:20
  418.8 7.8 %bitcast_reduce_fusion.2 = (f32[3,1024]{1,0:T(4,128)S(1)}, f32[3,1024,1024]{2,1,0:T(8,128)}) fusion(bf16[1024,3,128]{2,0,1:T(8,128)(2,1)} %get-tuple-element.182, bf16[16,1024,3,128]{3,1,0,2:T(8,128)(2,1)} %get-tuple-element.181, s32[]{:T(128)} %get-tuple-element.168), kind=kOutput, calls=%fused_computation.1.clone.1 | convolution fusion | flops 811594752 | bytes 14168576 | tf_op jit(solution)/shard_map/while/body/eval_jaxpr/qhd,khd->hqk/dot_general | solution.py:20
  440.1 7.8 %bitcast_reduce_fusion.2 = (f32[3,1024]{1,0:T(4,128)S(1)}, f32[3,1024,1024]{2,1,0:T(8,128)}) fusion(bf16[1024,3,128]{2,0,1:T(8,128)(2,1)} %get-tuple-element.182, bf16[16,1024,3,128]{3,1,0,2:T(8,128)(2,1)} %get-tuple-element.181, s32[]{:T(128)} %get-tuple-element.168), kind=kOutput, calls=%fused_computation.1.clone.1 | convolution fusion | flops 811594752 | bytes 14168576 | tf_op jit(solution)/shard_map/while/body/eval_jaxpr/qhd,khd->hqk/dot_general | solution.py:20
  461.3 7.8 %bitcast_reduce_fusion.2 = (f32[3,1024]{1,0:T(4,128)S(1)}, f32[3,1024,1024]{2,1,0:T(8,128)}) fusion(bf16[1024,3,128]{2,0,1:T(8,128)(2,1)} %get-tuple-element.182, bf16[16,1024,3,128]{3,1,0,2:T(8,128)(2,1)} %get-tuple-element.181, s32[]{:T(128)} %get-tuple-element.168), kind=kOutput, calls=%fused_computation.1.clone.1 | convolution fusion | flops 811594752 | bytes 14168576 | tf_op jit(solution)/shard_map/while/body/eval_jaxpr/qhd,khd->hqk/dot_general | solution.py:20
  482.6 7.8 %bitcast_reduce_fusion.2 = (f32[3,1024]{1,0:T(4,128)S(1)}, f32[3,1024,1024]{2,1,0:T(8,128)}) fusion(bf16[1024,3,128]{2,0,1:T(8,128)(2,1)} %get-tuple-element.182, bf16[16,1024,3,128]{3,1,0,2:T(8,128)(2,1)} %get-tuple-element.181, s32[]{:T(128)} %get-tuple-element.168), kind=kOutput, calls=%fused_computation.1.clone.1 | convolution fusion | flops 811594752 | bytes 14168576 | tf_op jit(solution)/shard_map/while/body/eval_jaxpr/qhd,khd->hqk/dot_general | solution.py:20
  503.9 7.8 %bitcast_reduce_fusion.2 = (f32[3,1024]{1,0:T(4,128)S(1)}, f32[3,1024,1024]{2,1,0:T(8,128)}) fusion(bf16[1024,3,128]{2,0,1:T(8,128)(2,1)} %get-tuple-element.182, bf16[16,1024,3,128]{3,1,0,2:T(8,128)(2,1)} %get-tuple-element.181, s32[]{:T(128)} %get-tuple-element.168), kind=kOutput, calls=%fused_computation.1.clone.1 | convolution fusion | flops 811594752 | bytes 14168576 | tf_op jit(solution)/shard_map/while/body/eval_jaxpr/qhd,khd->hqk/dot_general | solution.py:20
  525.2 7.8 %bitcast_reduce_fusion.2 = (f32[3,1024]{1,0:T(4,128)S(1)}, f32[3,1024,1024]{2,1,0:T(8,128)}) fusion(bf16[1024,3,128]{2,0,1:T(8,128)(2,1)} %get-tuple-element.182, bf16[16,1024,3,128]{3,1,0,2:T(8,128)(2,1)} %get-tuple-element.181, s32[]{:T(128)} %get-tuple-element.168), kind=kOutput, calls=%fused_computation.1.clone.1 | convolution fusion | flops 811594752 | bytes 14168576 | tf_op jit(solution)/shard_map/while/body/eval_jaxpr/qhd,khd->hqk/dot_general | solution.py:20
  548.9 21.4 %all_to_all.66 = bf16[8,128,384]{1,2,0:T(8,128)(2,1)S(1)} all-to-all(bf16[8,128,384]{1,2,0:T(8,128)(2,1)S(1)} %copy.42), channel_id=1, replica_groups=mesh['blk'=16,'head'=8] {'head'}, dimensions={0} | all-to-all | bytes 1572864 | tf_op jit(solution)/shard_map/all_to_all | solution.py:71
  (148 shorter events, 241.8 us)
Async XLA Ops:
  6.5 107.5 %all-gather.3.cloned.1.call-start = ((), (), s32[]{:S(2)}) async-start(), calls=%async_computation.4 | async-start | bytes 13369344 | tf_op jit(solution)/shard_map/all_gather | solution.py:56
  32.2 1.3 copy-start.2
  33.5 156.2 %all-gather.5.cloned.1.call-start = ((), (), s32[]{:S(2)}) async-start(), calls=%async_computation.5 | async-start | bytes 13369344 | tf_op jit(solution)/shard_map/all_gather | solution.py:57
  55.4 1.3 copy-start.1
  55.4 1.5 copy-start.3
  58.4 22.4 %all-to-all-start.1 = ((bf16[128,8,384]{0,2,1:T(8,128)(2,1)}), bf16[128,8,384]{0,2,1:T(8,128)(2,1)S(1)}, u32[]{:S(2)}, u32[]{:S(2)}) async-start(bf16[128,8,384]{0,2,1:T(8,128)(2,1)} %bitcast.3), calls=%async_computation.1 | async-start | bytes 1572864 | tf_op jit(solution)/shard_map/all_to_all | solution.py:43
  214.0 8.2 %copy-start = (f32[3,1024,1024]{2,1,0:T(8,128)S(1)}, f32[3,1024,1024]{2,1,0:T(8,128)}, u32[]{:S(2)}) copy-start(f32[3,1024,1024]{2,1,0:T(8,128)} %get-tuple-element.156) | copy-start | bytes 37748740 | tf_op jit(solution)/shard_map/while
  235.0 8.2 %copy-start = (f32[3,1024,1024]{2,1,0:T(8,128)S(1)}, f32[3,1024,1024]{2,1,0:T(8,128)}, u32[]{:S(2)}) copy-start(f32[3,1024,1024]{2,1,0:T(8,128)} %get-tuple-element.156) | copy-start | bytes 37748740 | tf_op jit(solution)/shard_map/while
  256.3 8.2 %copy-start = (f32[3,1024,1024]{2,1,0:T(8,128)S(1)}, f32[3,1024,1024]{2,1,0:T(8,128)}, u32[]{:S(2)}) copy-start(f32[3,1024,1024]{2,1,0:T(8,128)} %get-tuple-element.156) | copy-start | bytes 37748740 | tf_op jit(solution)/shard_map/while
  277.6 8.2 %copy-start = (f32[3,1024,1024]{2,1,0:T(8,128)S(1)}, f32[3,1024,1024]{2,1,0:T(8,128)}, u32[]{:S(2)}) copy-start(f32[3,1024,1024]{2,1,0:T(8,128)} %get-tuple-element.156) | copy-start | bytes 37748740 | tf_op jit(solution)/shard_map/while
  298.9 8.2 %copy-start = (f32[3,1024,1024]{2,1,0:T(8,128)S(1)}, f32[3,1024,1024]{2,1,0:T(8,128)}, u32[]{:S(2)}) copy-start(f32[3,1024,1024]{2,1,0:T(8,128)} %get-tuple-element.156) | copy-start | bytes 37748740 | tf_op jit(solution)/shard_map/while
  320.1 8.2 %copy-start = (f32[3,1024,1024]{2,1,0:T(8,128)S(1)}, f32[3,1024,1024]{2,1,0:T(8,128)}, u32[]{:S(2)}) copy-start(f32[3,1024,1024]{2,1,0:T(8,128)} %get-tuple-element.156) | copy-start | bytes 37748740 | tf_op jit(solution)/shard_map/while
  341.4 8.2 %copy-start = (f32[3,1024,1024]{2,1,0:T(8,128)S(1)}, f32[3,1024,1024]{2,1,0:T(8,128)}, u32[]{:S(2)}) copy-start(f32[3,1024,1024]{2,1,0:T(8,128)} %get-tuple-element.156) | copy-start | bytes 37748740 | tf_op jit(solution)/shard_map/while
  362.7 8.2 %copy-start = (f32[3,1024,1024]{2,1,0:T(8,128)S(1)}, f32[3,1024,1024]{2,1,0:T(8,128)}, u32[]{:S(2)}) copy-start(f32[3,1024,1024]{2,1,0:T(8,128)} %get-tuple-element.156) | copy-start | bytes 37748740 | tf_op jit(solution)/shard_map/while
  384.0 8.2 %copy-start = (f32[3,1024,1024]{2,1,0:T(8,128)S(1)}, f32[3,1024,1024]{2,1,0:T(8,128)}, u32[]{:S(2)}) copy-start(f32[3,1024,1024]{2,1,0:T(8,128)} %get-tuple-element.156) | copy-start | bytes 37748740 | tf_op jit(solution)/shard_map/while
  405.3 8.2 %copy-start = (f32[3,1024,1024]{2,1,0:T(8,128)S(1)}, f32[3,1024,1024]{2,1,0:T(8,128)}, u32[]{:S(2)}) copy-start(f32[3,1024,1024]{2,1,0:T(8,128)} %get-tuple-element.156) | copy-start | bytes 37748740 | tf_op jit(solution)/shard_map/while
  426.5 8.2 %copy-start = (f32[3,1024,1024]{2,1,0:T(8,128)S(1)}, f32[3,1024,1024]{2,1,0:T(8,128)}, u32[]{:S(2)}) copy-start(f32[3,1024,1024]{2,1,0:T(8,128)} %get-tuple-element.156) | copy-start | bytes 37748740 | tf_op jit(solution)/shard_map/while
  447.8 8.2 %copy-start = (f32[3,1024,1024]{2,1,0:T(8,128)S(1)}, f32[3,1024,1024]{2,1,0:T(8,128)}, u32[]{:S(2)}) copy-start(f32[3,1024,1024]{2,1,0:T(8,128)} %get-tuple-element.156) | copy-start | bytes 37748740 | tf_op jit(solution)/shard_map/while
  469.1 8.2 %copy-start = (f32[3,1024,1024]{2,1,0:T(8,128)S(1)}, f32[3,1024,1024]{2,1,0:T(8,128)}, u32[]{:S(2)}) copy-start(f32[3,1024,1024]{2,1,0:T(8,128)} %get-tuple-element.156) | copy-start | bytes 37748740 | tf_op jit(solution)/shard_map/while
  490.4 8.2 %copy-start = (f32[3,1024,1024]{2,1,0:T(8,128)S(1)}, f32[3,1024,1024]{2,1,0:T(8,128)}, u32[]{:S(2)}) copy-start(f32[3,1024,1024]{2,1,0:T(8,128)} %get-tuple-element.156) | copy-start | bytes 37748740 | tf_op jit(solution)/shard_map/while
  511.7 8.2 %copy-start = (f32[3,1024,1024]{2,1,0:T(8,128)S(1)}, f32[3,1024,1024]{2,1,0:T(8,128)}, u32[]{:S(2)}) copy-start(f32[3,1024,1024]{2,1,0:T(8,128)} %get-tuple-element.156) | copy-start | bytes 37748740 | tf_op jit(solution)/shard_map/while
  532.9 8.2 %copy-start = (f32[3,1024,1024]{2,1,0:T(8,128)S(1)}, f32[3,1024,1024]{2,1,0:T(8,128)}, u32[]{:S(2)}) copy-start(f32[3,1024,1024]{2,1,0:T(8,128)} %get-tuple-element.156) | copy-start | bytes 37748740 | tf_op jit(solution)/shard_map/while
Sparse Core Ops, SparseCore 0:
  33.6 80.3 all-gather.2
  115.7 73.9 all-gather.4
where the time goes:
time: 580 us; the launch traced here: 578 us
  matrix products  209 us (36%)
  other arithmetic  114 us (20%)
  waiting for transfers between devices  109 us (19%)
  blocking collectives  64.4 us (11%)
  local copies, waits for them, and re-layouts  63.7 us (11%)
  between operations  13.6 us (2%)
    dot_general x16, matrix products, absorb(): jnp.einsum('qhd,khd->hqk', q_heads, key_block, preferred_element_type=jnp...  124 us
    reduce_sum x16, other arithmetic, absorb(): new_sum = run_sum * shrink + jnp.sum(weights, axis=-1)  109 us
    dot_general x16, matrix products, absorb(): jnp.einsum('hqk,khd->hqd', weights.astype(jnp.bfloat16), value_block, pre...  85.5 us
    all_gather x1, waiting for transfers between devices, shards(): value_piece = lax.all_gather(v_heads, 'blk', axis=0, tiled=True)  59 us
    all_gather x1, waiting for transfers between devices, shards(): key_piece = lax.all_gather(k_heads, 'blk', axis=0, tiled=True)  31.2 us
    all_to_all x1, blocking collectives, shards(): lax.all_to_all(second_part, 'head', split_axis=1, concat_axis=0, tiled=True)  22 us
    all_to_all x1, blocking collectives, shards(): lax.all_to_all(result, 'head', split_axis=0, concat_axis=1, tiled=True)  21.4 us
    while x48, local copies, waits for them, and re-layouts  21.4 us
  transfers between devices with their start and end apart: 3, of which 3 were waited for; matrix products, arithmetic and copies ran while one was open for 4% of the time, Pallas kernels for 0%

commit v1 on v0

--- a/solution.py
+++ b/solution.py
@@ -53,8 +53,9 @@
         jnp.zeros((heads_here, rows), jnp.float32),
         jnp.zeros((heads_here, rows, HEAD_DIM), jnp.float32),
     )
-    key_piece = lax.all_gather(k_heads, "blk", axis=0, tiled=True)
-    value_piece = lax.all_gather(v_heads, "blk", axis=0, tiled=True)
+    w_next = jnp.concatenate([k_heads, v_heads], 1)
+    f_now = lax.all_gather(w_next, "blk", axis=0, tiled=True)
+    key_piece, value_piece = jnp.split(f_now, [k_heads.shape[1]], 1)
     length = key_piece.shape[0]
     block_rows = math.gcd(length, 1024)
     count = length // block_rows

time: 580 us -> 613 us (1.057)
  waiting for transfers between devices: 109 us -> 152 us
  blocking collectives: 64.4 us -> 22.1 us
  local copies, waits for them, and re-layouts: 63.7 us -> 81.7 us
  starting transfers between devices: 3.77 us -> 15.4 us
    split x0 -> x3, local copies, waits for them, and re-layouts: none -> 50.3 us  [shards(): key_piece, value_piece = jnp.split(f_now, [k_heads.shape[1]], 1)]
    all_to_all x2 -> x0, blocking collectives: 43 us -> none  [the longest x1 22 us: shards(): lax.all_to_all(second_part, 'head', split_axis=1, concat_axis=0, tiled=True)]
    all_gather x2 -> x0, local copies, waits for them, and re-layouts: 33.2 us -> none  [the longest x1 16.7 us: shards(): key_piece = lax.all_gather(k_heads, 'blk', axis=0, tiled=True)]
    all_to_all x0 -> x2, waiting for transfers between devices: none -> 24.9 us  [the longest x1 12.7 us: shards(): lax.all_to_all(values, 'head', split_axis=1, concat_axis=0, tiled=True)]
    all_gather x2 -> x1, waiting for transfers between devices: 90.1 us -> 107 us  [shards(): f_now = lax.all_gather(w_next, 'blk', axis=0, tiled=True)]
    all_to_all x0 -> x2, starting transfers between devices: none -> 11.6 us  [the longest x1 7.86 us: shards(): lax.all_to_all(second_part, 'head', split_axis=1, concat_axis=0, tiled=True)]
  transfers between devices with their start and end apart: 3 -> 4, of which waited for: 3 -> 4; matrix products, arithmetic and copies ran while one was open for 4% -> 1% of each run, Pallas kernels for 0% -> 0%
where the time goes in v1:
time: 613 us; the launch traced here: 611 us
  matrix products  210 us (34%)
  waiting for transfers between devices  152 us (25%)
  other arithmetic  116 us (19%)
  local copies, waits for them, and re-layouts  81.7 us (13%)
  blocking collectives  22.1 us (4%)
  starting transfers between devices  15.4 us (3%)
  between operations  13.5 us (2%)
    dot_general x16, matrix products, absorb(): jnp.einsum('qhd,khd->hqk', q_heads, key_block, preferred_element_type=jnp...  124 us
    reduce_sum x16, other arithmetic, absorb(): new_sum = run_sum * shrink + jnp.sum(weights, axis=-1)  109 us
    all_gather x1, waiting for transfers between devices, shards(): f_now = lax.all_gather(w_next, 'blk', axis=0, tiled=True)  107 us
    dot_general x16, matrix products, absorb(): jnp.einsum('hqk,khd->hqd', weights.astype(jnp.bfloat16), value_block, pre...  85.8 us
    split x3, local copies, waits for them, and re-layouts, shards(): key_piece, value_piece = jnp.split(f_now, [k_heads.shape[1]], 1)  50.3 us
    all_to_all x1, blocking collectives, shards(): lax.all_to_all(result, 'head', split_axis=0, concat_axis=1, tiled=True)  22.1 us
    while x48, local copies, waits for them, and re-layouts  21.4 us
    all_to_all x1, waiting for transfers between devices, shards(): lax.all_to_all(first_part, 'head', split_axis=1, concat_axis=0, tiled=True)  21 us
  transfers between devices with their start and end apart: 4, of which 4 were waited for; matrix products, arithmetic and copies ran while one was open for 1% of the time, Pallas kernels for 0%

profile of v1, /device:TPU:0, one launch (start us, length us, event | category | flops | bytes accessed | tf_op | source)
XLA Modules:
  0.0 611.0 jit_solution(6170507373256593090)
XLA Ops:
  10.5 7.9 %all-to-all-start = ((bf16[128,8,384]{0,2,1:T(8,128)(2,1)}), bf16[128,8,384]{0,2,1:T(8,128)(2,1)S(1)}, u32[]{:S(2)}, u32[]{:S(2)}) async-start(bf16[128,8,384]{0,2,1:T(8,128)(2,1)} %bitcast), calls=%async_computation | async-start | bytes 1572864 | tf_op jit(solution)/shard_map/all_to_all | solution.py:44
  19.5 12.2 %all-to-all-done = bf16[128,8,384]{0,2,1:T(8,128)(2,1)S(1)} async-done(((bf16[128,8,384]{0,2,1:T(8,128)(2,1)}), bf16[128,8,384]{0,2,1:T(8,128)(2,1)S(1)}, u32[]{:S(2)}, u32[]{:S(2)}) %all-to-all-start) | async-done | bytes 786464 | tf_op jit(solution)/shard_map/all_to_all | solution.py:44
  36.4 12.7 %all-to-all-done.1 = bf16[128,8,384]{0,2,1:T(8,128)(2,1)S(1)} async-done(((bf16[128,8,384]{0,2,1:T(8,128)(2,1)}), bf16[128,8,384]{0,2,1:T(8,128)(2,1)S(1)}, u32[]{:S(2)}, u32[]{:S(2)}) %all-to-all-start.1) | async-done | bytes 786464 | tf_op jit(solution)/shard_map/all_to_all | solution.py:45
  57.9 21.0 %all-to-all-done.2 = bf16[128,8,384]{0,2,1:T(8,128)(2,1)S(1)} async-done(((bf16[128,8,384]{0,2,1:T(8,128)(2,1)}), bf16[128,8,384]{0,2,1:T(8,128)(2,1)S(1)}, u32[]{:S(2)}, u32[]{:S(2)}) %all-to-all-start.2) | async-done | bytes 786464 | tf_op jit(solution)/shard_map/all_to_all | solution.py:43
  80.9 106.6 %all-gather.2.cloned.1.call-done = bf16[16384,6,128]{0,2,1:T(8,128)(2,1)} async-done(((bf16[1024,6,128]{0,2,1:T(8,128)(2,1)}), bf16[16384,6,128]{0,2,1:T(8,128)(2,1)}) %all-gather.2.cloned.1.call-update) | async-done | bytes 25165840 | tf_op jit(solution)/shard_map/all_gather | solution.py:57
  187.4 17.2 %fusion.26 = (bf16[16384,3,128]{0,2,1:T(8,128)(2,1)}, bf16[16384,3,128]{0,2,1:T(8,128)(2,1)}) fusion(bf16[16384,6,128]{0,2,1:T(8,128)(2,1)} %all-gather.2.cloned.1.call-done), kind=kLoop, calls=%fused_computation.37 | loop fusion | bytes 50331648 | tf_op jit(solution)/shard_map/split | solution.py:58
  204.6 16.5 %copy.34 = bf16[16384,3,128]{2,0,1:T(8,128)(2,1)} copy(bf16[16384,3,128]{0,2,1:T(8,128)(2,1)} %get-tuple-element.109) | data formatting | bytes 25165824 | tf_op jit(solution)/shard_map/split | solution.py:58
  221.1 16.6 %copy.37 = bf16[16384,3,128]{2,0,1:T(8,128)(2,1)} copy(bf16[16384,3,128]{0,2,1:T(8,128)(2,1)} %get-tuple-element.108) | data formatting | bytes 25165824 | tf_op jit(solution)/shard_map/split | solution.py:58
  237.7 340.8 %while.15 = (s32[]{:T(128)}, f32[3,1024]{1,0:T(4,128)S(1)}, f32[3,1024]{1,0:T(4,128)S(1)}, f32[3,1024,128]{2,1,0:T(8,128)}, bf16[16,1024,3,128]{3,1,0,2:T(8,128)...) while((s32[]{:T(128)}, f32[3,1024]{1,0:T(4,128)S(1)}, ...), condition=%wide.region_5.6_spmd.clone, body=%wide.region_2.5_spmd.clone.sunk | while | flops 1636973568 | bytes 93783168 | solution.py:68
  237.7 7.8 %bitcast_reduce_fusion.2 = (f32[3,1024]{1,0:T(4,128)S(1)}, f32[3,1024,1024]{2,1,0:T(8,128)}) fusion(bf16[1024,3,128]{2,0,1:T(8,128)(2,1)} %get-tuple-element.184, bf16[16,1024,3,128]{3,1,0,2:T(8,128)(2,1)} %get-tuple-element.183, s32[]{:T(128)} %get-tuple-element.170), kind=kOutput, calls=%fused_computation.1.clone.1 | convolution fusion | flops 811594752 | bytes 14168576 | tf_op jit(solution)/shard_map/while/body/eval_jaxpr/qhd,khd->hqk/dot_general | solution.py:20
  301.4 7.8 %bitcast_reduce_fusion.2 = (f32[3,1024]{1,0:T(4,128)S(1)}, f32[3,1024,1024]{2,1,0:T(8,128)}) fusion(bf16[1024,3,128]{2,0,1:T(8,128)(2,1)} %get-tuple-element.184, bf16[16,1024,3,128]{3,1,0,2:T(8,128)(2,1)} %get-tuple-element.183, s32[]{:T(128)} %get-tuple-element.170), kind=kOutput, calls=%fused_computation.1.clone.1 | convolution fusion | flops 811594752 | bytes 14168576 | tf_op jit(solution)/shard_map/while/body/eval_jaxpr/qhd,khd->hqk/dot_general | solution.py:20
  322.7 7.8 %bitcast_reduce_fusion.2 = (f32[3,1024]{1,0:T(4,128)S(1)}, f32[3,1024,1024]{2,1,0:T(8,128)}) fusion(bf16[1024,3,128]{2,0,1:T(8,128)(2,1)} %get-tuple-element.184, bf16[16,1024,3,128]{3,1,0,2:T(8,128)(2,1)} %get-tuple-element.183, s32[]{:T(128)} %get-tuple-element.170), kind=kOutput, calls=%fused_computation.1.clone.1 | convolution fusion | flops 811594752 | bytes 14168576 | tf_op jit(solution)/shard_map/while/body/eval_jaxpr/qhd,khd->hqk/dot_general | solution.py:20
  344.0 7.8 %bitcast_reduce_fusion.2 = (f32[3,1024]{1,0:T(4,128)S(1)}, f32[3,1024,1024]{2,1,0:T(8,128)}) fusion(bf16[1024,3,128]{2,0,1:T(8,128)(2,1)} %get-tuple-element.184, bf16[16,1024,3,128]{3,1,0,2:T(8,128)(2,1)} %get-tuple-element.183, s32[]{:T(128)} %get-tuple-element.170), kind=kOutput, calls=%fused_computation.1.clone.1 | convolution fusion | flops 811594752 | bytes 14168576 | tf_op jit(solution)/shard_map/while/body/eval_jaxpr/qhd,khd->hqk/dot_general | solution.py:20
  365.3 7.8 %bitcast_reduce_fusion.2 = (f32[3,1024]{1,0:T(4,128)S(1)}, f32[3,1024,1024]{2,1,0:T(8,128)}) fusion(bf16[1024,3,128]{2,0,1:T(8,128)(2,1)} %get-tuple-element.184, bf16[16,1024,3,128]{3,1,0,2:T(8,128)(2,1)} %get-tuple-element.183, s32[]{:T(128)} %get-tuple-element.170), kind=kOutput, calls=%fused_computation.1.clone.1 | convolution fusion | flops 811594752 | bytes 14168576 | tf_op jit(solution)/shard_map/while/body/eval_jaxpr/qhd,khd->hqk/dot_general | solution.py:20
  386.6 7.8 %bitcast_reduce_fusion.2 = (f32[3,1024]{1,0:T(4,128)S(1)}, f32[3,1024,1024]{2,1,0:T(8,128)}) fusion(bf16[1024,3,128]{2,0,1:T(8,128)(2,1)} %get-tuple-element.184, bf16[16,1024,3,128]{3,1,0,2:T(8,128)(2,1)} %get-tuple-element.183, s32[]{:T(128)} %get-tuple-element.170), kind=kOutput, calls=%fused_computation.1.clone.1 | convolution fusion | flops 811594752 | bytes 14168576 | tf_op jit(solution)/shard_map/while/body/eval_jaxpr/qhd,khd->hqk/dot_general | solution.py:20
  408.0 7.8 %bitcast_reduce_fusion.2 = (f32[3,1024]{1,0:T(4,128)S(1)}, f32[3,1024,1024]{2,1,0:T(8,128)}) fusion(bf16[1024,3,128]{2,0,1:T(8,128)(2,1)} %get-tuple-element.184, bf16[16,1024,3,128]{3,1,0,2:T(8,128)(2,1)} %get-tuple-element.183, s32[]{:T(128)} %get-tuple-element.170), kind=kOutput, calls=%fused_computation.1.clone.1 | convolution fusion | flops 811594752 | bytes 14168576 | tf_op jit(solution)/shard_map/while/body/eval_jaxpr/qhd,khd->hqk/dot_general | solution.py:20
  429.3 7.8 %bitcast_reduce_fusion.2 = (f32[3,1024]{1,0:T(4,128)S(1)}, f32[3,1024,1024]{2,1,0:T(8,128)}) fusion(bf16[1024,3,128]{2,0,1:T(8,128)(2,1)} %get-tuple-element.184, bf16[16,1024,3,128]{3,1,0,2:T(8,128)(2,1)} %get-tuple-element.183, s32[]{:T(128)} %get-tuple-element.170), kind=kOutput, calls=%fused_computation.1.clone.1 | convolution fusion | flops 811594752 | bytes 14168576 | tf_op jit(solution)/shard_map/while/body/eval_jaxpr/qhd,khd->hqk/dot_general | solution.py:20
  450.6 7.8 %bitcast_reduce_fusion.2 = (f32[3,1024]{1,0:T(4,128)S(1)}, f32[3,1024,1024]{2,1,0:T(8,128)}) fusion(bf16[1024,3,128]{2,0,1:T(8,128)(2,1)} %get-tuple-element.184, bf16[16,1024,3,128]{3,1,0,2:T(8,128)(2,1)} %get-tuple-element.183, s32[]{:T(128)} %get-tuple-element.170), kind=kOutput, calls=%fused_computation.1.clone.1 | convolution fusion | flops 811594752 | bytes 14168576 | tf_op jit(solution)/shard_map/while/body/eval_jaxpr/qhd,khd->hqk/dot_general | solution.py:20
  471.9 7.8 %bitcast_reduce_fusion.2 = (f32[3,1024]{1,0:T(4,128)S(1)}, f32[3,1024,1024]{2,1,0:T(8,128)}) fusion(bf16[1024,3,128]{2,0,1:T(8,128)(2,1)} %get-tuple-element.184, bf16[16,1024,3,128]{3,1,0,2:T(8,128)(2,1)} %get-tuple-element.183, s32[]{:T(128)} %get-tuple-element.170), kind=kOutput, calls=%fused_computation.1.clone.1 | convolution fusion | flops 811594752 | bytes 14168576 | tf_op jit(solution)/shard_map/while/body/eval_jaxpr/qhd,khd->hqk/dot_general | solution.py:20
  493.2 7.8 %bitcast_reduce_fusion.2 = (f32[3,1024]{1,0:T(4,128)S(1)}, f32[3,1024,1024]{2,1,0:T(8,128)}) fusion(bf16[1024,3,128]{2,0,1:T(8,128)(2,1)} %get-tuple-element.184, bf16[16,1024,3,128]{3,1,0,2:T(8,128)(2,1)} %get-tuple-element.183, s32[]{:T(128)} %get-tuple-element.170), kind=kOutput, calls=%fused_computation.1.clone.1 | convolution fusion | flops 811594752 | bytes 14168576 | tf_op jit(solution)/shard_map/while/body/eval_jaxpr/qhd,khd->hqk/dot_general | solution.py:20
  514.5 7.8 %bitcast_reduce_fusion.2 = (f32[3,1024]{1,0:T(4,128)S(1)}, f32[3,1024,1024]{2,1,0:T(8,128)}) fusion(bf16[1024,3,128]{2,0,1:T(8,128)(2,1)} %get-tuple-element.184, bf16[16,1024,3,128]{3,1,0,2:T(8,128)(2,1)} %get-tuple-element.183, s32[]{:T(128)} %get-tuple-element.170), kind=kOutput, calls=%fused_computation.1.clone.1 | convolution fusion | flops 811594752 | bytes 14168576 | tf_op jit(solution)/shard_map/while/body/eval_jaxpr/qhd,khd->hqk/dot_general | solution.py:20
  535.8 7.8 %bitcast_reduce_fusion.2 = (f32[3,1024]{1,0:T(4,128)S(1)}, f32[3,1024,1024]{2,1,0:T(8,128)}) fusion(bf16[1024,3,128]{2,0,1:T(8,128)(2,1)} %get-tuple-element.184, bf16[16,1024,3,128]{3,1,0,2:T(8,128)(2,1)} %get-tuple-element.183, s32[]{:T(128)} %get-tuple-element.170), kind=kOutput, calls=%fused_computation.1.clone.1 | convolution fusion | flops 811594752 | bytes 14168576 | tf_op jit(solution)/shard_map/while/body/eval_jaxpr/qhd,khd->hqk/dot_general | solution.py:20
  557.2 7.8 %bitcast_reduce_fusion.2 = (f32[3,1024]{1,0:T(4,128)S(1)}, f32[3,1024,1024]{2,1,0:T(8,128)}) fusion(bf16[1024,3,128]{2,0,1:T(8,128)(2,1)} %get-tuple-element.184, bf16[16,1024,3,128]{3,1,0,2:T(8,128)(2,1)} %get-tuple-element.183, s32[]{:T(128)} %get-tuple-element.170), kind=kOutput, calls=%fused_computation.1.clone.1 | convolution fusion | flops 811594752 | bytes 14168576 | tf_op jit(solution)/shard_map/while/body/eval_jaxpr/qhd,khd->hqk/dot_general | solution.py:20
  580.9 22.1 %all_to_all.64 = bf16[8,128,384]{1,2,0:T(8,128)(2,1)S(1)} all-to-all(bf16[8,128,384]{1,2,0:T(8,128)(2,1)S(1)} %copy.42), channel_id=1, replica_groups=mesh['blk'=16,'head'=8] {'head'}, dimensions={0} | all-to-all | bytes 1572864 | tf_op jit(solution)/shard_map/all_to_all | solution.py:72
  (149 shorter events, 255.9 us)
Async XLA Ops:
  9.3 9.0 %copy-start.2 = (bf16[128,3072]{1,0:T(8,128)(2,1)S(1)}, bf16[128,3072]{1,0:T(8,128)(2,1)}, u32[]{:S(2)}) copy-start(bf16[128,3072]{1,0:T(8,128)(2,1)} %param.9) | copy-start | bytes 2359300
  10.5 21.2 %all-to-all-start = ((bf16[128,8,384]{0,2,1:T(8,128)(2,1)}), bf16[128,8,384]{0,2,1:T(8,128)(2,1)S(1)}, u32[]{:S(2)}, u32[]{:S(2)}) async-start(bf16[128,8,384]{0,2,1:T(8,128)(2,1)} %bitcast), calls=%async_computation | async-start | bytes 1572864 | tf_op jit(solution)/shard_map/all_to_all | solution.py:44
  31.7 17.3 %all-to-all-start.1 = ((bf16[128,8,384]{0,2,1:T(8,128)(2,1)}), bf16[128,8,384]{0,2,1:T(8,128)(2,1)S(1)}, u32[]{:S(2)}, u32[]{:S(2)}) async-start(bf16[128,8,384]{0,2,1:T(8,128)(2,1)} %bitcast.2), calls=%async_computation.1 | async-start | bytes 1572864 | tf_op jit(solution)/shard_map/all_to_all | solution.py:45
  35.5 151.9 %all-gather.2.cloned.1.call-start = ((), (), s32[]{:S(2)}) async-start(), calls=%async_computation.4 | async-start | bytes 26738688 | tf_op jit(solution)/shard_map/all_gather | solution.py:57
  51.3 1.1 copy-start.1
  51.3 1.4 copy-start.3
  54.1 24.8 %all-to-all-start.2 = ((bf16[128,8,384]{0,2,1:T(8,128)(2,1)}), bf16[128,8,384]{0,2,1:T(8,128)(2,1)S(1)}, u32[]{:S(2)}, u32[]{:S(2)}) async-start(bf16[128,8,384]{0,2,1:T(8,128)(2,1)} %bitcast.5), calls=%async_computation.2 | async-start | bytes 1572864 | tf_op jit(solution)/shard_map/all_to_all | solution.py:43
  245.5 8.2 %copy-start = (f32[3,1024,1024]{2,1,0:T(8,128)S(1)}, f32[3,1024,1024]{2,1,0:T(8,128)}, u32[]{:S(2)}) copy-start(f32[3,1024,1024]{2,1,0:T(8,128)} %get-tuple-element.158) | copy-start | bytes 37748740 | tf_op jit(solution)/shard_map/while
  266.5 8.2 %copy-start = (f32[3,1024,1024]{2,1,0:T(8,128)S(1)}, f32[3,1024,1024]{2,1,0:T(8,128)}, u32[]{:S(2)}) copy-start(f32[3,1024,1024]{2,1,0:T(8,128)} %get-tuple-element.158) | copy-start | bytes 37748740 | tf_op jit(solution)/shard_map/while
  287.8 8.2 %copy-start = (f32[3,1024,1024]{2,1,0:T(8,128)S(1)}, f32[3,1024,1024]{2,1,0:T(8,128)}, u32[]{:S(2)}) copy-start(f32[3,1024,1024]{2,1,0:T(8,128)} %get-tuple-element.158) | copy-start | bytes 37748740 | tf_op jit(solution)/shard_map/while
  309.2 8.2 %copy-start = (f32[3,1024,1024]{2,1,0:T(8,128)S(1)}, f32[3,1024,1024]{2,1,0:T(8,128)}, u32[]{:S(2)}) copy-start(f32[3,1024,1024]{2,1,0:T(8,128)} %get-tuple-element.158) | copy-start | bytes 37748740 | tf_op jit(solution)/shard_map/while
  330.5 8.2 %copy-start = (f32[3,1024,1024]{2,1,0:T(8,128)S(1)}, f32[3,1024,1024]{2,1,0:T(8,128)}, u32[]{:S(2)}) copy-start(f32[3,1024,1024]{2,1,0:T(8,128)} %get-tuple-element.158) | copy-start | bytes 37748740 | tf_op jit(solution)/shard_map/while
  351.8 8.2 %copy-start = (f32[3,1024,1024]{2,1,0:T(8,128)S(1)}, f32[3,1024,1024]{2,1,0:T(8,128)}, u32[]{:S(2)}) copy-start(f32[3,1024,1024]{2,1,0:T(8,128)} %get-tuple-element.158) | copy-start | bytes 37748740 | tf_op jit(solution)/shard_map/while
  373.1 8.2 %copy-start = (f32[3,1024,1024]{2,1,0:T(8,128)S(1)}, f32[3,1024,1024]{2,1,0:T(8,128)}, u32[]{:S(2)}) copy-start(f32[3,1024,1024]{2,1,0:T(8,128)} %get-tuple-element.158) | copy-start | bytes 37748740 | tf_op jit(solution)/shard_map/while
  394.4 8.2 %copy-start = (f32[3,1024,1024]{2,1,0:T(8,128)S(1)}, f32[3,1024,1024]{2,1,0:T(8,128)}, u32[]{:S(2)}) copy-start(f32[3,1024,1024]{2,1,0:T(8,128)} %get-tuple-element.158) | copy-start | bytes 37748740 | tf_op jit(solution)/shard_map/while
  415.7 8.2 %copy-start = (f32[3,1024,1024]{2,1,0:T(8,128)S(1)}, f32[3,1024,1024]{2,1,0:T(8,128)}, u32[]{:S(2)}) copy-start(f32[3,1024,1024]{2,1,0:T(8,128)} %get-tuple-element.158) | copy-start | bytes 37748740 | tf_op jit(solution)/shard_map/while
  437.0 8.2 %copy-start = (f32[3,1024,1024]{2,1,0:T(8,128)S(1)}, f32[3,1024,1024]{2,1,0:T(8,128)}, u32[]{:S(2)}) copy-start(f32[3,1024,1024]{2,1,0:T(8,128)} %get-tuple-element.158) | copy-start | bytes 37748740 | tf_op jit(solution)/shard_map/while
  458.4 8.2 %copy-start = (f32[3,1024,1024]{2,1,0:T(8,128)S(1)}, f32[3,1024,1024]{2,1,0:T(8,128)}, u32[]{:S(2)}) copy-start(f32[3,1024,1024]{2,1,0:T(8,128)} %get-tuple-element.158) | copy-start | bytes 37748740 | tf_op jit(solution)/shard_map/while
  479.7 8.2 %copy-start = (f32[3,1024,1024]{2,1,0:T(8,128)S(1)}, f32[3,1024,1024]{2,1,0:T(8,128)}, u32[]{:S(2)}) copy-start(f32[3,1024,1024]{2,1,0:T(8,128)} %get-tuple-element.158) | copy-start | bytes 37748740 | tf_op jit(solution)/shard_map/while
  501.0 8.2 %copy-start = (f32[3,1024,1024]{2,1,0:T(8,128)S(1)}, f32[3,1024,1024]{2,1,0:T(8,128)}, u32[]{:S(2)}) copy-start(f32[3,1024,1024]{2,1,0:T(8,128)} %get-tuple-element.158) | copy-start | bytes 37748740 | tf_op jit(solution)/shard_map/while
  522.3 8.2 %copy-start = (f32[3,1024,1024]{2,1,0:T(8,128)S(1)}, f32[3,1024,1024]{2,1,0:T(8,128)}, u32[]{:S(2)}) copy-start(f32[3,1024,1024]{2,1,0:T(8,128)} %get-tuple-element.158) | copy-start | bytes 37748740 | tf_op jit(solution)/shard_map/while
  543.6 8.2 %copy-start = (f32[3,1024,1024]{2,1,0:T(8,128)S(1)}, f32[3,1024,1024]{2,1,0:T(8,128)}, u32[]{:S(2)}) copy-start(f32[3,1024,1024]{2,1,0:T(8,128)} %get-tuple-element.158) | copy-start | bytes 37748740 | tf_op jit(solution)/shard_map/while
  564.9 8.2 %copy-start = (f32[3,1024,1024]{2,1,0:T(8,128)S(1)}, f32[3,1024,1024]{2,1,0:T(8,128)}, u32[]{:S(2)}) copy-start(f32[3,1024,1024]{2,1,0:T(8,128)} %get-tuple-element.158) | copy-start | bytes 37748740 | tf_op jit(solution)/shard_map/while
Sparse Core Ops, SparseCore 0:
  51.4 135.9 all-gather.1
